TPU v7x, 32 devices: a whole 2x2x4 slice. The times are simulated.
32 devices in a mesh: rep: 4 (over y, x), shard: 2 (over core), exp: 4 (over z).
Axes of the slice: x: 2, y: 2, z: 4, core: 2. Of those that a mesh axis runs over, the one named last changes fastest.
Arguments:
- tokens: bfloat16 [2048, 2560], P(('rep', 'exp')), may hold values from -6 to 6
- expert_of: int32 [2048, 1], P(('rep', 'exp')), may hold values from 0 to 3; in each aligned block of 128 rows (0 to 127, 128 to 255, ...) at most 80 rows name the same one
- w_gate: bfloat16 [4, 768, 2560], P('exp', 'shard'), may hold values from -0.125 to 0.125
- w_up: bfloat16 [4, 768, 2560], P('exp', 'shard'), may hold values from -0.125 to 0.125
- d_hidden: bfloat16 [4, 4, 4, 80, 768], P('rep', 'exp', None, None, 'shard'), may hold values from -6 to 6
Outputs:
- hidden: bfloat16 [4, 4, 4, 80, 768], P('rep', 'exp', None, None, 'shard')
- d_tokens: bfloat16 [2048, 2560], P(('rep', 'exp'), 'shard')
- grad_gate: bfloat16 [4, 768, 2560], P('exp', 'shard')
- grad_up: bfloat16 [4, 768, 2560], P('exp', 'shard')
Inputs may be any that keep to these rules, and one draw needn't show every extreme that they name: `expert_of`: each value names an expert. Among the 128 tokens of one device (aligned blocks of rows), no expert is named more than 80 times, a bound that some block reaches.
All inputs are finite; a program needn't handle non-finite values.
Results may differ from a plain program's by a relative error of at most 0.017.
Values may be sent and summed in bfloat16 or wider, within the bound.
No kernel may reach another device: no remote copies, remote signals or barrier semaphores. Data moves between devices by JAX's collectives and lax.ppermute only.
A program may use at most 64 MiB of HBM per device.

v0:
```python
import jax
import jax.numpy as jnp
from jax import lax
from jax.sharding import PartitionSpec as P


def local(tokens, expert_of, w_gate, w_up, d_hidden):
    expert_count = lax.axis_size("exp")
    replica_count = lax.axis_size("rep")
    capacity = d_hidden.shape[3]
    feature_width = tokens.shape[1]
    slots_all = expert_count * capacity
    routed = expert_of[:, 0]
    chosen = (routed[:, None] == jnp.arange(expert_count, dtype=jnp.int32)[None, :]).astype(
        jnp.int32
    )
    slot_index = jnp.sum(chosen * (jnp.cumsum(chosen, axis=0) - 1), axis=1)
    target = routed * capacity + slot_index
    placing = (jnp.arange(slots_all, dtype=jnp.int32)[:, None] == target[None, :]).astype(
        jnp.bfloat16
    )
    packed = jnp.dot(placing, tokens, preferred_element_type=jnp.float32).astype(jnp.bfloat16)
    arrived = lax.all_to_all(
        packed.reshape(expert_count, capacity, feature_width),
        "exp",
        split_axis=0,
        concat_axis=0,
        tiled=True,
    )
    expert_rows = arrived.reshape(slots_all, feature_width)
    gate_rows = w_gate[0]
    up_rows = w_up[0]
    contract_last = (((1,), (1,)), ((), ()))
    gate_act = lax.dot_general(
        expert_rows, gate_rows, contract_last, preferred_element_type=jnp.float32
    )
    up_act = lax.dot_general(
        expert_rows, up_rows, contract_last, preferred_element_type=jnp.float32
    )
    sigma = jax.nn.sigmoid(gate_act)
    hidden = (gate_act * sigma * up_act).astype(jnp.bfloat16)
    cotan = d_hidden.reshape(slots_all, gate_rows.shape[0]).astype(jnp.float32)
    grad_gate_act = (cotan * up_act * sigma * (1.0 + gate_act * (1.0 - sigma))).astype(jnp.bfloat16)
    grad_up_act = (cotan * gate_act * sigma).astype(jnp.bfloat16)
    contract_first = (((0,), (0,)), ((), ()))
    part_gate = lax.dot_general(
        grad_gate_act, expert_rows, contract_first, preferred_element_type=jnp.float32
    )
    part_up = lax.dot_general(
        grad_up_act, expert_rows, contract_first, preferred_element_type=jnp.float32
    )
    total_gate, total_up = (
        lax.psum(
            part_gate.astype(jnp.bfloat16).astype(jnp.float32).astype(jnp.bfloat16), "rep"
        ).astype(jnp.float32),
        lax.psum(
            part_up.astype(jnp.bfloat16).astype(jnp.float32).astype(jnp.bfloat16), "rep"
        ).astype(jnp.float32),
    )
    grad_gate = (total_gate * (1.0 / replica_count)).astype(jnp.bfloat16)[None]
    grad_up = (total_up * (1.0 / replica_count)).astype(jnp.bfloat16)[None]
    partial_value = jnp.dot(grad_gate_act, gate_rows, preferred_element_type=jnp.float32)
    partial_value = partial_value + jnp.dot(
        grad_up_act, up_rows, preferred_element_type=jnp.float32
    )
    outgoing = partial_value.astype(jnp.bfloat16).reshape(expert_count, capacity, feature_width)
    returned = lax.all_to_all(outgoing, "exp", split_axis=0, concat_axis=0, tiled=True)
    unpacked = lax.dot_general(
        placing,
        returned.reshape(slots_all, feature_width),
        contract_first,
        preferred_element_type=jnp.float32,
    )
    d_tokens = lax.psum_scatter(
        unpacked.astype(jnp.bfloat16), "shard", scatter_dimension=1, tiled=True
    )
    return (hidden.reshape(d_hidden.shape), d_tokens, grad_gate, grad_up)


def solution(mesh):
    in_specs = (
        P(("rep", "exp"), None),
        P(("rep", "exp"), None),
        P("exp", "shard", None),
        P("exp", "shard", None),
        P("rep", "exp", None, None, "shard"),
    )
    out_specs = (
        P("rep", "exp", None, None, "shard"),
        P(("rep", "exp"), "shard"),
        P("exp", "shard", None),
        P("exp", "shard", None),
    )
    return jax.shard_map(local, mesh=mesh, in_specs=in_specs, out_specs=out_specs, check_vma=False)
```

profile of v0, /device:TPU:0, one launch (start us, length us, event | category | flops | bytes accessed | tf_op | source)
XLA Modules:
  0.0 176.9 jit_solution(2150093289877161744)
XLA Ops:
  8.0 0.0 copy-start
  8.0 0.0 all-reduce.3.cloned.1.call-start
  8.1 0.9 fusion.17
  8.9 0.2 reduce_window_sum.11
  9.1 0.8 select_reduce_fusion
  9.9 0.7 multiply_add_fusion
  10.6 1.7 convolution_convert_fusion.2
  12.3 0.0 copy-start.1
  12.3 44.6 %all_to_all.10 = bf16[4,80,2560]{2,1,0:T(8,128)(2,1)S(1)} all-to-all(bf16[4,80,2560]{2,1,0:T(8,128)(2,1)S(1)} %bitcast.39), channel_id=1, replica_groups=mesh['rep'=4,'shard'=2,'exp'=4] {'exp'}, dimensions={0} | all-to-all | bytes 3276800 | tf_op jit(solution)/shard_map/all_to_all | solution.py:23
  56.9 0.0 copy-done.1
  56.9 0.0 copy-start.2
  56.9 1.0 fusion.8
  57.9 0.0 copy-done
  57.9 0.0 copy-done.2
  57.9 1.9 %fusion.12 = (bf16[320,384]{1,0:T(8,128)(2,1)S(1)}, bf16[320,384]{1,0:T(8,128)(2,1)}, bf16[320,384]{1,0:T(8,128)(2,1)S(1)}) fusion(f32[320,384]{1,0:T(8,128)S(1)} %fusion.8, bf16[1,1,4,80,384]{4,3,2,1,0:T(8,128)(2,1)S(1)} %copy-done.2, bf16[320,2560]{1,0:T(8,128)(2,1)S(1)} %bitcast.41, bf16[1,384,2560]{2,1,0:T(8,128)(2,1)S(1)} %copy-done), kind=kOutput, calls=%fused_computation.21 | convolution fusion | flops 631234560 | bytes 5079040 | tf_op jit(solution)/shard_map/dot_general | solution.py:37
  59.8 2.5 %convolution_convert_fusion.1 = bf16[384,2560]{1,0:T(8,128)(2,1)} fusion(bf16[320,384]{1,0:T(8,128)(2,1)S(1)} %get-tuple-element.6, bf16[320,2560]{1,0:T(8,128)(2,1)S(1)} %bitcast.42), kind=kOutput, calls=%fused_computation.2 | convolution fusion | flops 630128640 | bytes 3850240 | tf_op jit(solution)/shard_map/dot_general | solution.py:46
  62.3 2.5 %convolution_convert_fusion = bf16[384,2560]{1,0:T(8,128)(2,1)} fusion(bf16[320,384]{1,0:T(8,128)(2,1)S(1)} %get-tuple-element.8, bf16[320,2560]{1,0:T(8,128)(2,1)S(1)} %bitcast.43), kind=kOutput, calls=%fused_computation.1 | convolution fusion | flops 630128640 | bytes 3850240 | tf_op jit(solution)/shard_map/dot_general | solution.py:49
  64.8 0.0 all-reduce.3.cloned.1.call-update
  64.8 0.0 reduce-scatter.2.cloned.1.call-start
  64.9 2.6 %fusion.6 = f32[320,2560]{1,0:T(8,128)S(1)} fusion(bf16[320,384]{1,0:T(8,128)(2,1)S(1)} %get-tuple-element.6, bf16[1,384,2560]{2,1,0:T(8,128)(2,1)} %param.7), kind=kOutput, calls=%fused_computation.13 | convolution fusion | flops 629145600 | bytes 5488640 | tf_op jit(solution)/shard_map/dot_general | solution.py:62
  67.4 1.0 fusion
  68.5 40.2 %all_to_all.11 = bf16[4,80,2560]{2,1,0:T(8,128)(2,1)S(1)} all-to-all(bf16[4,80,2560]{2,1,0:T(8,128)(2,1)S(1)} %bitcast.37), channel_id=1, replica_groups=mesh['rep'=4,'shard'=2,'exp'=4] {'exp'}, dimensions={0} | all-to-all | bytes 3276800 | tf_op jit(solution)/shard_map/all_to_all | solution.py:67
  108.7 1.4 convolution_convert_fusion.3
  110.1 0.0 reduce-scatter.2.cloned.1.call-update
  110.1 54.6 %all-reduce.3.cloned.1.call-done = (bf16[384,2560]{1,0:T(8,128)(2,1)}, bf16[384,2560]{1,0:T(8,128)(2,1)}) async-done(((bf16[384,2560]{1,0:T(8,128)(2,1)}, bf16[384,2560]{1,0:T(8,128)(2,1)}), (bf16[384,2560]{1,0:T(8,128)(2,1)}, bf16[384,2560]{1,0:T(8,128)(2,1)})) %all-reduce.3.cloned.1.call-update) | async-done | bytes 3932176 | tf_op jit(solution)/shard_map/psum | solution.py:53
  164.7 4.7 %fusion.1 = (bf16[1,384,2560]{2,1,0:T(8,128)(2,1)}, bf16[1,384,2560]{2,1,0:T(8,128)(2,1)}) fusion(bf16[384,2560]{1,0:T(8,128)(2,1)} %get-tuple-element.4, bf16[384,2560]{1,0:T(8,128)(2,1)} %get-tuple-element.5), kind=kLoop, calls=%fused_computation.8 | loop fusion | flops 5898240 | bytes 7864320 | tf_op jit(solution)/shard_map/broadcast_in_dim | solution.py:60
  169.4 0.0 reduce-scatter.2.cloned.1.call-done
Async XLA Ops:
  8.0 49.9 %copy-start = (bf16[1,384,2560]{2,1,0:T(8,128)(2,1)S(1)}, bf16[1,384,2560]{2,1,0:T(8,128)(2,1)}, u32[]{:S(2)}) copy-start(bf16[1,384,2560]{2,1,0:T(8,128)(2,1)} %param.8) | copy-start | bytes 5898244
  8.0 156.7 %all-reduce.3.cloned.1.call-start = ((), (), s32[]{:S(2)}) async-start(), calls=%async_computation.4 | async-start | bytes 7864320 | tf_op jit(solution)/shard_map/psum | solution.py:53
  12.3 44.6 %copy-start.1 = (bf16[1,384,2560]{2,1,0:T(8,128)(2,1)S(1)}, bf16[1,384,2560]{2,1,0:T(8,128)(2,1)}, u32[]{:S(2)}) copy-start(bf16[1,384,2560]{2,1,0:T(8,128)(2,1)} %param.7) | copy-start | bytes 5898244
  56.9 1.0 copy-start.2
  64.8 104.6 %reduce-scatter.2.cloned.1.call-start = ((), (), s32[]{:S(2)}) async-start(), calls=%async_computation.3 | async-start | bytes 983040 | tf_op jit(solution)/shard_map/reduce_scatter | solution.py:74
Sparse Core Ops, SparseCore 0:
  64.9 99.7 all-reduce.2
Sparse Core Ops, SparseCore 1:
  110.2 7.1 reduce-scatter.1
where the time goes:
time: 177 us
  blocking collectives  84.9 us (48%)
  waiting for transfers between devices  54.6 us (31%)
  between operations  15.5 us (9%)
  matrix products  14.5 us (8%)
  other arithmetic  7.28 us (4%)
    psum x1, waiting for transfers between devices, local(): lax.psum(part_gate.astype(jnp.bfloat16).astype(jnp.float32).astype(jnp.bf...  54.6 us
    all_to_all x1, blocking collectives, local(): lax.all_to_all(packed.reshape(expert_count, capacity, feature_width), 'ex...  44.6 us
    all_to_all x1, blocking collectives, local(): lax.all_to_all(outgoing, 'exp', split_axis=0, concat_axis=0, tiled=True)  40.2 us
    broadcast_in_dim x1, other arithmetic, local(): grad_gate = (total_gate * (1.0 / replica_count)).astype(jnp.bfloat16)[None]  4.75 us
  transfers between devices with their start and end apart: 2, of which 1 were waited for; matrix products, arithmetic and copies ran while one was open for 5% of the time, Pallas kernels for 0%

commit v1 on v0

--- a/solution.py
+++ b/solution.py
@@ -20,13 +20,20 @@
         jnp.bfloat16
     )
     packed = jnp.dot(placing, tokens, preferred_element_type=jnp.float32).astype(jnp.bfloat16)
-    arrived = lax.all_to_all(
-        packed.reshape(expert_count, capacity, feature_width),
-        "exp",
-        split_axis=0,
-        concat_axis=0,
-        tiled=True,
-    )
+    x = packed.reshape(expert_count, capacity, feature_width)
+    ways, here = (lax.axis_size("exp"), lax.axis_index("exp"))
+    width = x.shape[0] // ways
+    dims = list(x.shape)
+    dims[0] = width
+    height = dims[0]
+    dims[0] = height * ways
+    full = jnp.zeros(dims, x.dtype)
+    for mask in range(ways):
+        part = lax.dynamic_slice_in_dim(x, (here ^ mask) * width, width, axis=0)
+        if mask:
+            part = lax.ppermute(part, "exp", [(d, d ^ mask) for d in range(ways)])
+        full = lax.dynamic_update_slice_in_dim(full, part, (here ^ mask) * height, axis=0)
+    arrived = full
     expert_rows = arrived.reshape(slots_all, feature_width)
     gate_rows = w_gate[0]
     up_rows = w_up[0]

time: 177 us -> 177 us (level)
  blocking collectives: 84.9 us -> 47.2 us
  waiting for transfers between devices: 54.6 us -> 83.2 us
  starting transfers between devices: 0.08 us -> 5.75 us
    all_to_all x1 -> x0, blocking collectives: 44.6 us -> none  [local(): lax.all_to_all(packed.reshape(expert_count, capacity, feature_width), 'ex...]
    ppermute x0 -> x3, waiting for transfers between devices: none -> 28.2 us  [local(): part = lax.ppermute(part, 'exp', [(d, d ^ mask) for d in range(ways)])]
    all_to_all x1, blocking collectives: 40.2 us -> 47.2 us  [local(): lax.all_to_all(outgoing, 'exp', split_axis=0, concat_axis=0, tiled=True)]
    ppermute x0 -> x3, starting transfers between devices: none -> 5.67 us  [local(): part = lax.ppermute(part, 'exp', [(d, d ^ mask) for d in range(ways)])]
  transfers between devices with their start and end apart: 2 -> 5, of which waited for: 1 -> 3; matrix products, arithmetic and copies ran while one was open for 5% -> 6% of each run, Pallas kernels for 0% -> 0%
where the time goes in v1:
time: 177 us; the launch traced here: 176 us
  waiting for transfers between devices  83.2 us (47%)
  blocking collectives  47.2 us (27%)
  matrix products  15.7 us (9%)
  between operations  15.6 us (9%)
  other arithmetic  7.28 us (4%)
  starting transfers between devices  5.75 us (3%)
    psum x1, waiting for transfers between devices, local(): lax.psum(part_gate.astype(jnp.bfloat16).astype(jnp.float32).astype(jnp.bf...  55 us
    all_to_all x1, blocking collectives, local(): lax.all_to_all(outgoing, 'exp', split_axis=0, concat_axis=0, tiled=True)  47.2 us
    ppermute x3, waiting for transfers between devices, local(): part = lax.ppermute(part, 'exp', [(d, d ^ mask) for d in range(ways)])  28.2 us
    ppermute x3, starting transfers between devices, local(): part = lax.ppermute(part, 'exp', [(d, d ^ mask) for d in range(ways)])  5.67 us
    broadcast_in_dim x1, other arithmetic, local(): grad_gate = (total_gate * (1.0 / replica_count)).astype(jnp.bfloat16)[None]  4.75 us
  transfers between devices with their start and end apart: 5, of which 3 were waited for; matrix products, arithmetic and copies ran while one was open for 6% of the time, Pallas kernels for 0%

profile of v1, /device:TPU:0, one launch (start us, length us, event | category | flops | bytes accessed | tf_op | source)
XLA Modules:
  0.0 176.4 jit_solution(16181398130571000451)
XLA Ops:
  8.0 0.0 copy-start
  8.0 0.0 all-reduce.3.cloned.1.call-start
  8.1 0.9 fusion.17
  8.9 0.2 reduce_window_sum.11
  9.1 0.8 select_reduce_fusion
  9.9 0.7 multiply_add_fusion
  10.6 2.8 %convolution_convert_fusion.2 = bf16[320,2560]{1,0:T(8,128)(2,1)} fusion(bf16[128,2560]{1,0:T(8,128)(2,1)} %param.5, s32[128]{0:T(128)S(1)} %multiply_add_fusion), kind=kOutput, calls=%fused_computation.4 | convolution fusion | flops 210575360 | bytes 2294272 | tf_op jit(solution)/shard_map/dot_general | solution.py:22
  13.4 0.1 broadcast_in_dim.12
  13.6 1.3 copy-done.1
  14.9 0.1 constant_dynamic-slice_fusion.2
  15.0 0.0 copy-start.2
  15.0 3.1 %collective-permute-start = (bf16[1,80,2560]{2,1,0:T(8,128)(2,1)S(1)}, bf16[1,80,2560]{2,1,0:T(8,128)(2,1)S(1)}, u32[]{:S(2)}, u32[]{:S(2)}) collective-permute-start(bf16[1,80,2560]{2,1,0:T(8,128)(2,1)S(1)} %get-tuple-element.8), channel_id=1, source_target_pairs={{0,1},{1,0},{2,3},{3,2},{4,5},{5,4},{6,7},{7,6},{8,9},{9,8},{10,11... | collective-permute-start | bytes 1228808 | tf_op jit(solution)/shard_map/ppermute | solution.py:34
  18.1 2.6 %collective-permute-start.1 = (bf16[1,80,2560]{2,1,0:T(8,128)(2,1)S(1)}, bf16[1,80,2560]{2,1,0:T(8,128)(2,1)S(1)}, u32[]{:S(2)}, u32[]{:S(2)}) collective-permute-start(bf16[1,80,2560]{2,1,0:T(8,128)(2,1)S(1)} %get-tuple-element.7), channel_id=1, source_target_pairs={{0,2},{1,3},{2,0},{3,1},{4,6},{5,7},{6,4},{7,5},{8,10},{9,11},{10,... | collective-permute-start | bytes 1228808 | tf_op jit(solution)/shard_map/ppermute | solution.py:34
  20.7 0.0 collective-permute-start.2
  20.7 14.9 %collective-permute-done = bf16[1,80,2560]{2,1,0:T(8,128)(2,1)S(1)} collective-permute-done((bf16[1,80,2560]{2,1,0:T(8,128)(2,1)S(1)}, bf16[1,80,2560]{2,1,0:T(8,128)(2,1)S(1)}, u32[]{:S(2)}, u32[]{:S(2)}) %collective-permute-start) | collective-permute-done | bytes 409632 | tf_op jit(solution)/shard_map/ppermute | solution.py:34
  35.6 13.3 %collective-permute-done.1 = bf16[1,80,2560]{2,1,0:T(8,128)(2,1)S(1)} collective-permute-done((bf16[1,80,2560]{2,1,0:T(8,128)(2,1)S(1)}, bf16[1,80,2560]{2,1,0:T(8,128)(2,1)S(1)}, u32[]{:S(2)}, u32[]{:S(2)}) %collective-permute-start.1) | collective-permute-done | bytes 409632 | tf_op jit(solution)/shard_map/ppermute | solution.py:34
  49.0 0.0 collective-permute-done.2
  49.0 0.0 copy-done.2
  49.0 0.0 copy-start.3
  49.1 1.0 fusion.8
  50.1 1.9 %fusion.12 = (bf16[320,384]{1,0:T(8,128)(2,1)S(1)}, bf16[320,384]{1,0:T(8,128)(2,1)}, bf16[320,384]{1,0:T(8,128)(2,1)S(1)}) fusion(f32[320,384]{1,0:T(8,128)S(1)} %fusion.8, bf16[1,1,4,80,384]{4,3,2,1,0:T(8,128)(2,1)S(1)} %copy-done.3, bf16[320,2560]{1,0:T(8,128)(2,1)S(1)} %bitcast.41, bf16[1,384,2560]{2,1,0:T(8,128)(2,1)S(1)} %copy-done), kind=kOutput, calls=%fused_computation.21 | convolution fusion | flops 631234560 | bytes 5079040 | tf_op jit(solution)/shard_map/dot_general | solution.py:44
  52.0 2.5 %convolution_convert_fusion.1 = bf16[384,2560]{1,0:T(8,128)(2,1)} fusion(bf16[320,384]{1,0:T(8,128)(2,1)S(1)} %get-tuple-element.10, bf16[320,2560]{1,0:T(8,128)(2,1)S(1)} %bitcast.42), kind=kOutput, calls=%fused_computation.2 | convolution fusion | flops 630128640 | bytes 3850240 | tf_op jit(solution)/shard_map/dot_general | solution.py:53
  54.5 2.5 %convolution_convert_fusion = bf16[384,2560]{1,0:T(8,128)(2,1)} fusion(bf16[320,384]{1,0:T(8,128)(2,1)S(1)} %get-tuple-element.12, bf16[320,2560]{1,0:T(8,128)(2,1)S(1)} %bitcast.43), kind=kOutput, calls=%fused_computation.1 | convolution fusion | flops 630128640 | bytes 3850240 | tf_op jit(solution)/shard_map/dot_general | solution.py:56
  57.0 0.0 all-reduce.3.cloned.1.call-update
  57.0 0.0 reduce-scatter.2.cloned.1.call-start
  57.0 2.6 %fusion.6 = f32[320,2560]{1,0:T(8,128)S(1)} fusion(bf16[320,384]{1,0:T(8,128)(2,1)S(1)} %get-tuple-element.10, bf16[1,384,2560]{2,1,0:T(8,128)(2,1)} %param.7), kind=kOutput, calls=%fused_computation.13 | convolution fusion | flops 629145600 | bytes 5488640 | tf_op jit(solution)/shard_map/dot_general | solution.py:69
  59.6 1.0 fusion
  60.6 47.2 %all_to_all.5 = bf16[4,80,2560]{2,1,0:T(8,128)(2,1)S(1)} all-to-all(bf16[4,80,2560]{2,1,0:T(8,128)(2,1)S(1)} %bitcast.37), channel_id=1, replica_groups=mesh['rep'=4,'shard'=2,'exp'=4] {'exp'}, dimensions={0} | all-to-all | bytes 3276800 | tf_op jit(solution)/shard_map/all_to_all | solution.py:74
  107.8 1.4 convolution_convert_fusion.3
  109.2 0.0 reduce-scatter.2.cloned.1.call-update
  109.2 55.0 %all-reduce.3.cloned.1.call-done = (bf16[384,2560]{1,0:T(8,128)(2,1)}, bf16[384,2560]{1,0:T(8,128)(2,1)}) async-done(((bf16[384,2560]{1,0:T(8,128)(2,1)}, bf16[384,2560]{1,0:T(8,128)(2,1)}), (bf16[384,2560]{1,0:T(8,128)(2,1)}, bf16[384,2560]{1,0:T(8,128)(2,1)})) %all-reduce.3.cloned.1.call-update) | async-done | bytes 3932176 | tf_op jit(solution)/shard_map/psum | solution.py:60
  164.2 4.7 %fusion.1 = (bf16[1,384,2560]{2,1,0:T(8,128)(2,1)}, bf16[1,384,2560]{2,1,0:T(8,128)(2,1)}) fusion(bf16[384,2560]{1,0:T(8,128)(2,1)} %get-tuple-element.4, bf16[384,2560]{1,0:T(8,128)(2,1)} %get-tuple-element.5), kind=kLoop, calls=%fused_computation.8 | loop fusion | flops 5898240 | bytes 7864320 | tf_op jit(solution)/shard_map/broadcast_in_dim | solution.py:67
  (7 shorter events, 0.1 us)
Async XLA Ops:
  8.0 42.1 %copy-start = (bf16[1,384,2560]{2,1,0:T(8,128)(2,1)S(1)}, bf16[1,384,2560]{2,1,0:T(8,128)(2,1)}, u32[]{:S(2)}) copy-start(bf16[1,384,2560]{2,1,0:T(8,128)(2,1)} %param.8) | copy-start | bytes 5898244
  8.0 156.2 %all-reduce.3.cloned.1.call-start = ((), (), s32[]{:S(2)}) async-start(), calls=%async_computation.3 | async-start | bytes 7864320 | tf_op jit(solution)/shard_map/psum | solution.py:60
  13.4 1.4 copy-start.1
  15.0 34.0 %copy-start.2 = (bf16[1,384,2560]{2,1,0:T(8,128)(2,1)S(1)}, bf16[1,384,2560]{2,1,0:T(8,128)(2,1)}, u32[]{:S(2)}) copy-start(bf16[1,384,2560]{2,1,0:T(8,128)(2,1)} %param.7) | copy-start | bytes 5898244
  15.0 20.6 %collective-permute-start = (bf16[1,80,2560]{2,1,0:T(8,128)(2,1)S(1)}, bf16[1,80,2560]{2,1,0:T(8,128)(2,1)S(1)}, u32[]{:S(2)}, u32[]{:S(2)}) collective-permute-start(bf16[1,80,2560]{2,1,0:T(8,128)(2,1)S(1)} %get-tuple-element.8), channel_id=1, source_target_pairs={{0,1},{1,0},{2,3},{3,2},{4,5},{5,4},{6,7},{7,6},{8,9},{9,8},{10,11... | collective-permute-start | bytes 1228808 | tf_op jit(solution)/shard_map/ppermute | solution.py:34
  18.1 30.8 %collective-permute-start.1 = (bf16[1,80,2560]{2,1,0:T(8,128)(2,1)S(1)}, bf16[1,80,2560]{2,1,0:T(8,128)(2,1)S(1)}, u32[]{:S(2)}, u32[]{:S(2)}) collective-permute-start(bf16[1,80,2560]{2,1,0:T(8,128)(2,1)S(1)} %get-tuple-element.7), channel_id=1, source_target_pairs={{0,2},{1,3},{2,0},{3,1},{4,6},{5,7},{6,4},{7,5},{8,10},{9,11},{10,... | collective-permute-start | bytes 1228808 | tf_op jit(solution)/shard_map/ppermute | solution.py:34
  20.7 28.3 %collective-permute-start.2 = (bf16[1,80,2560]{2,1,0:T(8,128)(2,1)S(1)}, bf16[1,80,2560]{2,1,0:T(8,128)(2,1)S(1)}, u32[]{:S(2)}, u32[]{:S(2)}) collective-permute-start(bf16[1,80,2560]{2,1,0:T(8,128)(2,1)S(1)} %get-tuple-element.6), channel_id=1, source_target_pairs={{0,3},{1,2},{2,1},{3,0},{4,7},{5,6},{6,5},{7,4},{8,11},{9,10},{10,... | collective-permute-start | bytes 1228808 | tf_op jit(solution)/shard_map/ppermute | solution.py:34
  49.0 1.1 copy-start.3
  57.0 112.0 %reduce-scatter.2.cloned.1.call-start = ((), (), s32[]{:S(2)}) async-start(), calls=%async_computation.2 | async-start | bytes 983040 | tf_op jit(solution)/shard_map/reduce_scatter | solution.py:81
Sparse Core Ops, SparseCore 0:
  57.1 107.0 all-reduce.2
Sparse Core Ops, SparseCore 1:
  109.3 7.1 reduce-scatter.1
